TPU v7x, 32 devices: a whole 2x2x4 slice. The times are simulated.
32 devices in a mesh: ctx: 16 (over z, y, core), tp: 2 (over x).
Axes of the slice: x: 2, y: 2, z: 4, core: 2. Of those that a mesh axis runs over, the one named last changes fastest.
Arguments:
- activations: bfloat16 [2048, 4096], P(('ctx', 'tp')), may hold values from -24 to 24
- query_weight: bfloat16 [4096, 4096], P(None, 'tp'), may hold values from -0.09375 to 0.09375
- key_weight: bfloat16 [4096, 1024], P(None, 'tp'), may hold values from -0.09375 to 0.09375
- value_weight: bfloat16 [4096, 1024], P(None, 'tp'), may hold values from -0.09375 to 0.09375
Outputs:
- attended: bfloat16 [2048, 4096], P('ctx', 'tp')
All inputs are finite; a program needn't handle non-finite values.
Results may differ from a plain program's by a relative error of at most 0.012.
The roundings to bfloat16 on the way count: a program that leaves them out, or rounds other values in their place, can miss the bound.
Values may be sent and summed in bfloat16 or wider, within the bound.
No kernel may reach another device: no remote copies, remote signals or barrier semaphores. Data moves between devices by JAX's collectives and lax.ppermute only.
A program may use at most 128 MiB of HBM per device.

v0:
```python
import math
import jax
import jax.numpy as jnp
from jax import lax
from jax.sharding import PartitionSpec as P

HD = 128
THETA = 500000.0
NEGATIVE = -1e30


def rotate(heads_in, positions):
    width = heads_in.shape[-1]
    half_width = width // 2
    frequency = THETA ** (-(jnp.arange(half_width).astype(jnp.float32) * 2.0 / width))
    angles = positions[:, None] * frequency[None, :]
    cosine = jnp.cos(angles)[:, None, :]
    sine_table = jnp.sin(angles)[:, None, :]
    front_half = heads_in[..., :half_width]
    back_half = heads_in[..., half_width:]
    return jnp.concatenate(
        [
            front_half * cosine - back_half * sine_table,
            back_half * cosine + front_half * sine_table,
        ],
        axis=-1,
    )


def block_update(state, query_block, query_pos, key_block, value_block, key_pos):
    row_top, totals, accum = state
    scale = 1.0 / math.sqrt(query_block.shape[-1])
    scores = (
        lax.dot_general(
            query_block, key_block, (((1,), (1,)), ((), ())), preferred_element_type=jnp.float32
        )
        * scale
    )
    allowed = key_pos[None, :] <= query_pos[:, None]
    block_top = jnp.max(jnp.where(allowed, scores, NEGATIVE), axis=1)
    new_top = jnp.maximum(row_top, block_top)
    correction = jnp.exp(row_top - new_top)
    weights = jnp.where(allowed, jnp.exp(scores - new_top[:, None]), 0.0)
    totals = totals * correction + jnp.sum(weights, axis=1)
    accum = accum * correction[:, None] + jnp.dot(
        weights.astype(jnp.bfloat16), value_block, preferred_element_type=jnp.float32
    )
    return (new_top, totals, accum)


def attend(groups, keys, values):
    carry_start = []
    for query_rows, query_pos, kv_slot, query_step in groups:
        row_count = query_rows.shape[0]
        blocks_count = row_count // query_step
        carry_start.append(
            (
                jnp.full((blocks_count, query_step), NEGATIVE, jnp.float32),
                jnp.zeros((blocks_count, query_step), jnp.float32),
                jnp.zeros((blocks_count, query_step, HD), jnp.float32),
            )
        )
    carry = tuple(carry_start)
    key_piece = lax.all_gather(keys, "ctx", axis=0, tiled=True)
    value_piece = lax.all_gather(values, "ctx", axis=0, tiled=True)
    piece_rows = key_piece.shape[0]
    key_step = math.gcd(piece_rows, 512)
    updated = []
    for (query_rows, query_pos, kv_slot, query_step), fold_state in zip(groups, carry):
        key_chosen = lax.dynamic_index_in_dim(
            key_piece.reshape(piece_rows, -1, HD), kv_slot, 1, keepdims=False
        )
        value_chosen = lax.dynamic_index_in_dim(
            value_piece.reshape(piece_rows, -1, HD), kv_slot, 1, keepdims=False
        )
        key_blocks = key_chosen.reshape(piece_rows // key_step, key_step, HD)
        value_blocks = value_chosen.reshape(piece_rows // key_step, key_step, HD)
        block_starts = jnp.arange(piece_rows // key_step, dtype=jnp.int32) * key_step
        blocks_count = fold_state[0].shape[0]
        query_blocks = query_rows.reshape(blocks_count, query_step, HD)
        pos_blocks = query_pos.reshape(blocks_count, query_step)

        def per_query(items):
            query_block, pos_block, row_top, totals, accum = items
            last_pos = jnp.max(pos_block)

            def per_key(inner, key_items):
                key_block, value_block, key_start = key_items
                key_pos = key_start + jnp.arange(key_step, dtype=jnp.int32)
                result = lax.cond(
                    key_start <= last_pos,
                    lambda current: block_update(
                        current, query_block, pos_block, key_block, value_block, key_pos
                    ),
                    lambda current: current,
                    inner,
                )
                return (result, None)

            final, unused = lax.scan(
                per_key, (row_top, totals, accum), (key_blocks, value_blocks, block_starts)
            )
            return final

        updated.append(
            lax.map(
                per_query, (query_blocks, pos_blocks, fold_state[0], fold_state[1], fold_state[2])
            )
        )
    final_state = tuple(updated)
    results = []
    for state in final_state:
        outcome = state[2] / state[1][..., None]
        results.append(outcome.reshape(-1, HD))
    return results


def local(activations, query_weight, key_weight, value_weight):
    tensor_count = lax.axis_size("tp")
    context_index = lax.axis_index("ctx")
    local_rows = activations.shape[0] * tensor_count
    heads_here = query_weight.shape[1] // HD
    kv_here = key_weight.shape[1] // HD
    group = heads_here // kv_here
    query_width = heads_here * HD
    key_width = kv_here * HD
    gathered = lax.all_gather(activations, "tp", axis=0, tiled=True)
    projected = jnp.concatenate(
        [
            jnp.dot(gathered, query_weight, preferred_element_type=jnp.float32),
            jnp.dot(gathered, key_weight, preferred_element_type=jnp.float32),
            jnp.dot(gathered, value_weight, preferred_element_type=jnp.float32),
        ],
        axis=1,
    )
    token_pos = context_index * local_rows + jnp.arange(local_rows, dtype=jnp.int32)
    positions = token_pos.astype(jnp.float32)
    queries = rotate(
        projected[:, :query_width].reshape(local_rows, heads_here, HD), positions
    ).astype(jnp.bfloat16)
    keys = (
        rotate(
            projected[:, query_width : query_width + key_width].reshape(local_rows, kv_here, HD),
            positions,
        )
        .astype(jnp.bfloat16)
        .reshape(local_rows, key_width)
    )
    values = projected[:, query_width + key_width :].astype(jnp.bfloat16)
    groups = []
    for kv_slot in range(kv_here):
        chosen = queries[:, kv_slot * group : (kv_slot + 1) * group].reshape(local_rows * group, HD)
        groups.append(
            (chosen, jnp.repeat(token_pos, group), kv_slot, math.gcd(local_rows * group, 512))
        )
    results = attend(groups, keys, values)
    pieces = [outcome.astype(jnp.bfloat16).reshape(local_rows, group * HD) for outcome in results]
    return jnp.concatenate(pieces, axis=1)


def solution(mesh):
    in_specs = (P(("ctx", "tp"), None), P(None, "tp"), P(None, "tp"), P(None, "tp"))
    out_specs = P("ctx", "tp")
    return jax.shard_map(local, mesh=mesh, in_specs=in_specs, out_specs=out_specs, check_vma=False)
```

profile of v0, /device:TPU:25, one launch (start us, length us, event | category | flops | bytes accessed | tf_op | source)
XLA Modules:
  0.0 219.5 jit_solution(12466268835597819170)
XLA Ops:
  7.6 23.6 %all-gather.4.cloned.1.call-done = bf16[128,4096]{1,0:T(8,128)(2,1)} async-done(((bf16[64,4096]{1,0:T(8,128)(2,1)}), bf16[128,4096]{1,0:T(8,128)(2,1)}) %all-gather.4.cloned.1.call-update) | async-done | bytes 1048592 | tf_op jit(solution)/shard_map/all_gather | solution.py:127
  31.2 3.3 %fusion.78 = f32[128,512]{1,0:T(8,128)S(1)} fusion(bf16[128,4096]{1,0:T(8,128)(2,1)} %all-gather.4.cloned.1.call-done, bf16[4096,512]{1,0:T(8,128)(2,1)} %param.22), kind=kOutput, calls=%fused_computation.123 | convolution fusion | flops 536870912 | bytes 5505024 | tf_op jit(solution)/shard_map/dot_general | solution.py:131
  36.0 3.6 %convolution_convert_fusion = bf16[128,512]{1,0:T(8,128)(2,1)} fusion(bf16[128,4096]{1,0:T(8,128)(2,1)S(1)} %copy-done, bf16[4096,512]{1,0:T(8,128)(2,1)} %param.23), kind=kOutput, calls=%fused_computation.93 | convolution fusion | flops 536936448 | bytes 5373952 | tf_op jit(solution)/shard_map/dot_general | solution.py:132
  40.3 8.2 %convolution_bitcast_fusion = f32[16,8,16,128]{3,1,2,0:T(8,128)S(1)} fusion(bf16[128,4096]{1,0:T(8,128)(2,1)S(1)} %copy-done, bf16[4096,2048]{1,0:T(8,128)(2,1)} %param.21), kind=kOutput, calls=%fused_computation.92 | convolution fusion | flops 2147483648 | bytes 18874368 | tf_op jit(solution)/shard_map/dot_general | solution.py:130
  50.6 25.6 %all-gather.6.cloned.1.call-done = bf16[2048,512]{0,1:T(8,128)(2,1)} async-done(((bf16[128,512]{0,1:T(8,128)(2,1)}), bf16[2048,512]{0,1:T(8,128)(2,1)}) %all-gather.6.cloned.1.call-update) | async-done | bytes 2097168 | tf_op jit(solution)/shard_map/all_gather | solution.py:64
  76.1 2.7 %fusion.77 = (bf16[2048,1,128]{0,2,1:T(8,128)(2,1)S(1)}, bf16[2048,1,128]{0,2,1:T(8,128)(2,1)}, bf16[2048,1,128]{0,2,1:T(8,128)(2,1)}, bf16[2048,1,128]{0,2,1:T(8,128)(2,1)}) fusion(bf16[2048,4,128]{0,2,1:T(8,128)(2,1)} %bitcast.80), kind=kLoop, calls=%fused_computation.122 | loop fusion | bytes 4194304 | tf_op jit(solution)/shard_map/jit(dynamic_index_in_dim)/dynamic_slice | solution.py:70
  79.9 39.1 %all-gather.8.cloned.1.call-done = bf16[2048,512]{1,0:T(8,128)(2,1)} async-done(((bf16[128,512]{1,0:T(8,128)(2,1)}), bf16[2048,512]{1,0:T(8,128)(2,1)}) %all-gather.8.cloned.1.call-update) | async-done | bytes 2097168 | tf_op jit(solution)/shard_map/all_gather | solution.py:65
  121.5 4.0 %fusion.76 = (bf16[2048,1,128]{2,1,0:T(2,128)(2,1)S(1)}, bf16[2048,1,128]{2,1,0:T(2,128)(2,1)}, bf16[2048,1,128]{2,1,0:T(2,128)(2,1)}, bf16[2048,1,128]{2,1,0:T(2,128)(2,1)S(1)}) fusion(bf16[2048,4,128]{2,1,0:T(4,128)(2,1)S(1)} %reshape.177), kind=kLoop, calls=%fused_computation.121 | loop fusion | bytes 4194304 | tf_op jit(solution)/shard_map/jit(dynamic_index_in_dim)/dynamic_slice | solution.py:73
  126.5 22.5 %while.96 = (s32[]{:T(128)}, f32[512]{0:T(512)S(1)}, f32[512]{0:T(512)S(1)}, f32[512,128]{1,0:T(8,128)S(1)}, s32[4]{0:T(128)S(1)}, /*index=5*/s32[]{:T(128)}, bf...) while((s32[]{:T(128)}, f32[512]{0:T(512)S(1)}, ...), condition=%wide.region_6.7_spmd.clone, body=%wide.region_1.0_spmd.clone.sunk | while | flops 137496064 | bytes 4122387 | solution.py:100
  128.3 3.8 %conditional.12 = ((f32[512]{0:T(512)S(1)}, f32[512]{0:T(512)S(1)}, f32[512,128]{1,0:T(8,128)S(1)})) conditional(s32[]{:T(128)} %convert_element_type.119, (f32[512]{0:T(512)S(1)}, f32[512]{0:T(512)S(1)}, f32[512,128]{1,0:T(8,128)S(1)}) %tuple.163, (s32[]{:T(128)}, s32[512]{0:T(512)S(1)}, s32[128]{0:T(128)S(1)}, bf16[4,512,128]{2,1,0:T(8,128)(2,1)}, ...), branch_computations={%region_2.2_spmd, %region_3.5_spmd} | conditional | flops 137496064 | bytes 4120100 | solution.py:90
  133.9 3.8 %conditional.12 = ((f32[512]{0:T(512)S(1)}, f32[512]{0:T(512)S(1)}, f32[512,128]{1,0:T(8,128)S(1)})) conditional(s32[]{:T(128)} %convert_element_type.119, (f32[512]{0:T(512)S(1)}, f32[512]{0:T(512)S(1)}, f32[512,128]{1,0:T(8,128)S(1)}) %tuple.163, (s32[]{:T(128)}, s32[512]{0:T(512)S(1)}, s32[128]{0:T(128)S(1)}, bf16[4,512,128]{2,1,0:T(8,128)(2,1)}, ...), branch_computations={%region_2.2_spmd, %region_3.5_spmd} | conditional | flops 137496064 | bytes 4120100 | solution.py:90
  139.5 3.8 %conditional.12 = ((f32[512]{0:T(512)S(1)}, f32[512]{0:T(512)S(1)}, f32[512,128]{1,0:T(8,128)S(1)})) conditional(s32[]{:T(128)} %convert_element_type.119, (f32[512]{0:T(512)S(1)}, f32[512]{0:T(512)S(1)}, f32[512,128]{1,0:T(8,128)S(1)}) %tuple.163, (s32[]{:T(128)}, s32[512]{0:T(512)S(1)}, s32[128]{0:T(128)S(1)}, bf16[4,512,128]{2,1,0:T(8,128)(2,1)}, ...), branch_computations={%region_2.2_spmd, %region_3.5_spmd} | conditional | flops 137496064 | bytes 4120100 | solution.py:90
  145.2 3.8 %conditional.12 = ((f32[512]{0:T(512)S(1)}, f32[512]{0:T(512)S(1)}, f32[512,128]{1,0:T(8,128)S(1)})) conditional(s32[]{:T(128)} %convert_element_type.119, (f32[512]{0:T(512)S(1)}, f32[512]{0:T(512)S(1)}, f32[512,128]{1,0:T(8,128)S(1)}) %tuple.163, (s32[]{:T(128)}, s32[512]{0:T(512)S(1)}, s32[128]{0:T(128)S(1)}, bf16[4,512,128]{2,1,0:T(8,128)(2,1)}, ...), branch_computations={%region_2.2_spmd, %region_3.5_spmd} | conditional | flops 137496064 | bytes 4120100 | solution.py:90
  151.2 23.1 %while.97 = (s32[]{:T(128)}, f32[512]{0:T(512)S(1)}, f32[512]{0:T(512)S(1)}, f32[512,128]{1,0:T(8,128)S(1)}, s32[4]{0:T(128)S(1)}, /*index=5*/s32[]{:T(128)}, bf...) while((s32[]{:T(128)}, f32[512]{0:T(512)S(1)}, ...), condition=%wide.region_12.13_spmd.clone, body=%wide.region_7.12_spmd.clone.sunk | while | flops 137496064 | bytes 4122387 | solution.py:100
  153.1 3.9 %conditional.13 = ((f32[512]{0:T(512)S(1)}, f32[512]{0:T(512)S(1)}, f32[512,128]{1,0:T(8,128)S(1)})) conditional(s32[]{:T(128)} %convert_element_type.120, (f32[512]{0:T(512)S(1)}, f32[512]{0:T(512)S(1)}, f32[512,128]{1,0:T(8,128)S(1)}) %tuple.166, (s32[]{:T(128)}, s32[512]{0:T(512)S(1)}, s32[128]{0:T(128)S(1)}, bf16[4,512,128]{2,1,0:T(8,128)(2,1)}, ...), branch_computations={%region_8.8_spmd, %region_9.11_spmd} | conditional | flops 137496064 | bytes 4120100 | solution.py:90
  158.9 3.9 %conditional.13 = ((f32[512]{0:T(512)S(1)}, f32[512]{0:T(512)S(1)}, f32[512,128]{1,0:T(8,128)S(1)})) conditional(s32[]{:T(128)} %convert_element_type.120, (f32[512]{0:T(512)S(1)}, f32[512]{0:T(512)S(1)}, f32[512,128]{1,0:T(8,128)S(1)}) %tuple.166, (s32[]{:T(128)}, s32[512]{0:T(512)S(1)}, s32[128]{0:T(128)S(1)}, bf16[4,512,128]{2,1,0:T(8,128)(2,1)}, ...), branch_computations={%region_8.8_spmd, %region_9.11_spmd} | conditional | flops 137496064 | bytes 4120100 | solution.py:90
  164.7 3.9 %conditional.13 = ((f32[512]{0:T(512)S(1)}, f32[512]{0:T(512)S(1)}, f32[512,128]{1,0:T(8,128)S(1)})) conditional(s32[]{:T(128)} %convert_element_type.120, (f32[512]{0:T(512)S(1)}, f32[512]{0:T(512)S(1)}, f32[512,128]{1,0:T(8,128)S(1)}) %tuple.166, (s32[]{:T(128)}, s32[512]{0:T(512)S(1)}, s32[128]{0:T(128)S(1)}, bf16[4,512,128]{2,1,0:T(8,128)(2,1)}, ...), branch_computations={%region_8.8_spmd, %region_9.11_spmd} | conditional | flops 137496064 | bytes 4120100 | solution.py:90
  170.4 3.9 %conditional.13 = ((f32[512]{0:T(512)S(1)}, f32[512]{0:T(512)S(1)}, f32[512,128]{1,0:T(8,128)S(1)})) conditional(s32[]{:T(128)} %convert_element_type.120, (f32[512]{0:T(512)S(1)}, f32[512]{0:T(512)S(1)}, f32[512,128]{1,0:T(8,128)S(1)}) %tuple.166, (s32[]{:T(128)}, s32[512]{0:T(512)S(1)}, s32[128]{0:T(128)S(1)}, bf16[4,512,128]{2,1,0:T(8,128)(2,1)}, ...), branch_computations={%region_8.8_spmd, %region_9.11_spmd} | conditional | flops 137496064 | bytes 4120100 | solution.py:90
  175.7 19.9 %while.98 = (s32[]{:T(128)}, f32[512]{0:T(512)S(1)}, f32[512]{0:T(512)S(1)}, f32[512,128]{1,0:T(8,128)S(1)}, s32[4]{0:T(128)S(1)}, /*index=5*/s32[]{:T(128)}, bf...) while((s32[]{:T(128)}, f32[512]{0:T(512)S(1)}, ...), condition=%wide.region_18.19_spmd.clone, body=%wide.region_13.18_spmd.clone.sunk | while | flops 137496064 | bytes 4121879 | solution.py:100
  177.8 2.9 %conditional.14 = ((f32[512]{0:T(512)S(1)}, f32[512]{0:T(512)S(1)}, f32[512,128]{1,0:T(8,128)S(1)})) conditional(s32[]{:T(128)} %convert_element_type.121, (f32[512]{0:T(512)S(1)}, f32[512]{0:T(512)S(1)}, f32[512,128]{1,0:T(8,128)S(1)}) %tuple.169, (s32[]{:T(128)}, s32[512]{0:T(512)S(1)}, s32[128]{0:T(128)S(1)}, bf16[4,512,128]{2,1,0:T(8,128)(2,1)}, ...), branch_computations={%region_14.14_spmd, %region_15.17_spmd} | conditional | flops 137496064 | bytes 4119592 | solution.py:90
  182.7 2.9 %conditional.14 = ((f32[512]{0:T(512)S(1)}, f32[512]{0:T(512)S(1)}, f32[512,128]{1,0:T(8,128)S(1)})) conditional(s32[]{:T(128)} %convert_element_type.121, (f32[512]{0:T(512)S(1)}, f32[512]{0:T(512)S(1)}, f32[512,128]{1,0:T(8,128)S(1)}) %tuple.169, (s32[]{:T(128)}, s32[512]{0:T(512)S(1)}, s32[128]{0:T(128)S(1)}, bf16[4,512,128]{2,1,0:T(8,128)(2,1)}, ...), branch_computations={%region_14.14_spmd, %region_15.17_spmd} | conditional | flops 137496064 | bytes 4119592 | solution.py:90
  187.7 2.9 %conditional.14 = ((f32[512]{0:T(512)S(1)}, f32[512]{0:T(512)S(1)}, f32[512,128]{1,0:T(8,128)S(1)})) conditional(s32[]{:T(128)} %convert_element_type.121, (f32[512]{0:T(512)S(1)}, f32[512]{0:T(512)S(1)}, f32[512,128]{1,0:T(8,128)S(1)}) %tuple.169, (s32[]{:T(128)}, s32[512]{0:T(512)S(1)}, s32[128]{0:T(128)S(1)}, bf16[4,512,128]{2,1,0:T(8,128)(2,1)}, ...), branch_computations={%region_14.14_spmd, %region_15.17_spmd} | conditional | flops 137496064 | bytes 4119592 | solution.py:90
  192.7 2.9 %conditional.14 = ((f32[512]{0:T(512)S(1)}, f32[512]{0:T(512)S(1)}, f32[512,128]{1,0:T(8,128)S(1)})) conditional(s32[]{:T(128)} %convert_element_type.121, (f32[512]{0:T(512)S(1)}, f32[512]{0:T(512)S(1)}, f32[512,128]{1,0:T(8,128)S(1)}) %tuple.169, (s32[]{:T(128)}, s32[512]{0:T(512)S(1)}, s32[128]{0:T(128)S(1)}, bf16[4,512,128]{2,1,0:T(8,128)(2,1)}, ...), branch_computations={%region_14.14_spmd, %region_15.17_spmd} | conditional | flops 137496064 | bytes 4119592 | solution.py:90
  196.3 15.6 %while.99 = (s32[]{:T(128)}, f32[512]{0:T(512)S(1)}, f32[512]{0:T(512)S(1)}, f32[512,128]{1,0:T(8,128)S(1)}, s32[4]{0:T(128)S(1)}, /*index=5*/s32[]{:T(128)}, bf...) while((s32[]{:T(128)}, f32[512]{0:T(512)S(1)}, ...), condition=%wide.region_24.25_spmd.clone, body=%wide.region_19.24_spmd.clone.sunk | while | flops 137496064 | bytes 4121371 | solution.py:100
  (240 shorter events, 82.3 us)
Async XLA Ops:
  6.5 24.7 %all-gather.4.cloned.1.call-start = ((), (), s32[]{:S(2)}) async-start(), calls=%async_computation | async-start | bytes 1572864 | tf_op jit(solution)/shard_map/all_gather | solution.py:127
  7.3 68.9 %all-gather.6.cloned.1.call-start = ((), (), s32[]{:S(2)}) async-start(), calls=%async_computation.1 | async-start | bytes 2228224 | tf_op jit(solution)/shard_map/all_gather | solution.py:64
  31.2 4.8 %copy-start = (bf16[128,4096]{1,0:T(8,128)(2,1)S(1)}, bf16[128,4096]{1,0:T(8,128)(2,1)}, u32[]{:S(2)}) copy-start(bf16[128,4096]{1,0:T(8,128)(2,1)} %all-gather.4.cloned.1.call-done) | copy-start | bytes 3145732
  35.9 83.1 %all-gather.8.cloned.1.call-start = ((), (), s32[]{:S(2)}) async-start(), calls=%async_computation.2 | async-start | bytes 2228224 | tf_op jit(solution)/shard_map/all_gather | solution.py:65
  126.5 22.7 %copy-start.5 = (bf16[2048,1,128]{0,2,1:T(8,128)(2,1)S(1)}, bf16[2048,1,128]{0,2,1:T(8,128)(2,1)}, u32[]{:S(2)}) copy-start(bf16[2048,1,128]{0,2,1:T(8,128)(2,1)} %get-tuple-element.984) | copy-start | bytes 1572868
  126.5 23.7 %copy-start.2 = (bf16[2048,1,128]{2,1,0:T(2,128)(2,1)S(1)}, bf16[2048,1,128]{2,1,0:T(2,128)(2,1)}, u32[]{:S(2)}) copy-start(bf16[2048,1,128]{2,1,0:T(2,128)(2,1)} %get-tuple-element.979) | copy-start | bytes 1572868
  151.2 23.4 %copy-start.4 = (bf16[2048,1,128]{0,2,1:T(8,128)(2,1)S(1)}, bf16[2048,1,128]{0,2,1:T(8,128)(2,1)}, u32[]{:S(2)}) copy-start(bf16[2048,1,128]{0,2,1:T(8,128)(2,1)} %get-tuple-element.983) | copy-start | bytes 1572868
  151.2 24.4 %copy-start.1 = (bf16[2048,1,128]{2,1,0:T(2,128)(2,1)S(1)}, bf16[2048,1,128]{2,1,0:T(2,128)(2,1)}, u32[]{:S(2)}) copy-start(bf16[2048,1,128]{2,1,0:T(2,128)(2,1)} %get-tuple-element.978) | copy-start | bytes 1572868
  175.7 20.1 %copy-start.3 = (bf16[2048,1,128]{0,2,1:T(8,128)(2,1)S(1)}, bf16[2048,1,128]{0,2,1:T(8,128)(2,1)}, u32[]{:S(2)}) copy-start(bf16[2048,1,128]{0,2,1:T(8,128)(2,1)} %get-tuple-element.982) | copy-start | bytes 1572868
Sparse Core Ops, SparseCore 0:
  8.9 22.2 all-gather.3
  36.0 40.0 all-gather.5
  78.3 40.6 all-gather.7
where the time goes:
time: 221 us; the launch traced here: 219 us
  waiting for transfers between devices  89 us (40%)
  matrix products  47.3 us (21%)
  local copies, waits for them, and re-layouts  28.9 us (13%)
  loops' own time  21.6 us (10%)
  other arithmetic  19.1 us (9%)
  between operations  13.5 us (6%)
    all_gather x1, waiting for transfers between devices, attend(): value_piece = lax.all_gather(values, 'ctx', axis=0, tiled=True)  39.1 us
    all_gather x1, waiting for transfers between devices, attend(): key_piece = lax.all_gather(keys, 'ctx', axis=0, tiled=True)  25.6 us
    all_gather x1, waiting for transfers between devices, local(): gathered = lax.all_gather(activations, 'tp', axis=0, tiled=True)  23.6 us
    another operation x4, loops' own time, per_query(): lax.scan(per_key, (row_top, totals, accum), (key_blocks, value_blocks, bl...  20.8 us
    dot_general x16, matrix products, block_update(): lax.dot_general(query_block, key_block, (((1,), (1,)), ((), ())), preferr...  16.5 us
    dot_general x16, matrix products, block_update(): jnp.dot(weights.astype(jnp.bfloat16), value_block, preferred_element_type...  15.7 us
    add x16, other arithmetic, per_key(): key_pos = key_start + jnp.arange(key_step, dtype=jnp.int32)  10.2 us
    dynamic_slice x16, local copies, waits for them, and re-layouts, per_query(): lax.scan(per_key, (row_top, totals, accum), (key_blocks, value_blocks, bl...  9.76 us
  transfers between devices with their start and end apart: 3, of which 3 were waited for; matrix products, arithmetic and copies ran while one was open for 8% of the time, Pallas kernels for 0%

commit v1 on v0

--- a/solution.py
+++ b/solution.py
@@ -61,7 +61,17 @@
             )
         )
     carry = tuple(carry_start)
-    key_piece = lax.all_gather(keys, "ctx", axis=0, tiled=True)
+    everything, carry_in = (jax.lax.axis_size("ctx"), jax.lax.axis_index("ctx"))
+    key_piece, work_now = (keys, 1)
+    while work_now < everything:
+        log = []
+        for k0 in tuple(range(everything)):
+            log.append((k0, k0 ^ work_now))
+        arr_out = jax.lax.ppermute(key_piece, "ctx", perm=log)
+        y = jnp.concatenate([key_piece, arr_out], axis=0)
+        b_next = jnp.concatenate([arr_out, key_piece], axis=0)
+        key_piece = jnp.where(carry_in & work_now == 0, y, b_next)
+        work_now = 2 * work_now
     value_piece = lax.all_gather(values, "ctx", axis=0, tiled=True)
     piece_rows = key_piece.shape[0]
     key_step = math.gcd(piece_rows, 512)

time: 221 us -> 217 us (0.982)
  local copies, waits for them, and re-layouts: 28.9 us -> 24.5 us
  matrix products: 47.3 us -> 44.3 us
  starting transfers between devices: 0.08 us -> 2.43 us
    ppermute x0 -> x4, waiting for transfers between devices: none -> 64.5 us  [attend(): arr_out = jax.lax.ppermute(key_piece, 'ctx', perm=log)]
    all_gather x1, waiting for transfers between devices: 39.1 us -> 0.01 us  [attend(): value_piece = lax.all_gather(values, 'ctx', axis=0, tiled=True)]
    all_gather x1 -> x0, waiting for transfers between devices: 25.6 us -> none  [attend(): key_piece = lax.all_gather(keys, 'ctx', axis=0, tiled=True)]
    dot_general x16, matrix products: 15.7 us -> 8.27 us  [block_update(): jnp.dot(weights.astype(jnp.bfloat16), value_block, preferred_element_type...]
    unnamed x21 -> x11, local copies, waits for them, and re-layouts: 5.44 us -> 0.48 us
    reshape x0 -> x1, matrix products: none -> 3.93 us  [local(): projected[:, query_width:query_width + key_width]]
    dot_general x16, matrix products: 16.5 us -> 19.9 us  [block_update(): lax.dot_general(query_block, key_block, (((1,), (1,)), ((), ())), preferr...]
    dot_general x1 -> x0, matrix products: 3.31 us -> none  [local(): jnp.dot(gathered, key_weight, preferred_element_type=jnp.float32)]
  transfers between devices with their start and end apart: 3 -> 6, of which waited for: 3 -> 5; matrix products, arithmetic and copies ran while one was open for 8% -> 10% of each run, Pallas kernels for 0% -> 0%
where the time goes in v1:
time: 217 us; the launch traced here: 216 us
  waiting for transfers between devices  88.9 us (41%)
  matrix products  44.3 us (20%)
  local copies, waits for them, and re-layouts  24.5 us (11%)
  loops' own time  21.2 us (10%)
  other arithmetic  20.4 us (9%)
  between operations  13.8 us (6%)
  starting transfers between devices  2.43 us (1%)
    ppermute x4, waiting for transfers between devices, attend(): arr_out = jax.lax.ppermute(key_piece, 'ctx', perm=log)  64.5 us
    all_gather x1, waiting for transfers between devices, local(): gathered = lax.all_gather(activations, 'tp', axis=0, tiled=True)  23.7 us
    another operation x4, loops' own time, per_query(): lax.scan(per_key, (row_top, totals, accum), (key_blocks, value_blocks, bl...  20.5 us
    dot_general x16, matrix products, block_update(): lax.dot_general(query_block, key_block, (((1,), (1,)), ((), ())), preferr...  19.9 us
    add x16, other arithmetic, per_key(): key_pos = key_start + jnp.arange(key_step, dtype=jnp.int32)  10.4 us
    dynamic_slice x16, local copies, waits for them, and re-layouts, per_query(): lax.scan(per_key, (row_top, totals, accum), (key_blocks, value_blocks, bl...  9.49 us
    dot_general x16, matrix products, block_update(): jnp.dot(weights.astype(jnp.bfloat16), value_block, preferred_element_type...  8.27 us
    dot_general x1, matrix products, local(): jnp.dot(gathered, query_weight, preferred_element_type=jnp.float32)  8.22 us
  transfers between devices with their start and end apart: 6, of which 5 were waited for; matrix products, arithmetic and copies ran while one was open for 10% of the time, Pallas kernels for 0%

profile of v1, /device:TPU:25, one launch (start us, length us, event | category | flops | bytes accessed | tf_op | source)
XLA Modules:
  0.0 215.6 jit_solution(2414004716501961658)
XLA Ops:
  7.5 23.7 %all-gather.3.cloned.1.call-done = bf16[128,4096]{1,0:T(8,128)(2,1)} async-done(((bf16[64,4096]{1,0:T(8,128)(2,1)}), bf16[128,4096]{1,0:T(8,128)(2,1)}) %all-gather.3.cloned.1.call-update) | async-done | bytes 1048592 | tf_op jit(solution)/shard_map/all_gather | solution.py:137
  31.2 4.0 %convolution_convert_fusion = bf16[128,512]{1,0:T(8,128)(2,1)} fusion(bf16[128,4096]{1,0:T(8,128)(2,1)} %all-gather.3.cloned.1.call-done, bf16[4096,512]{1,0:T(8,128)(2,1)} %param.23), kind=kOutput, calls=%fused_computation.94 | convolution fusion | flops 536936448 | bytes 5373952 | tf_op jit(solution)/shard_map/dot_general | solution.py:142
  35.2 3.9 %fusion.78 = f32[128,512]{0,1:T(8,128)S(1)} fusion(bf16[128,4096]{1,0:T(8,128)(2,1)S(1)} %copy-done, bf16[4096,512]{1,0:T(8,128)(2,1)} %param.22), kind=kOutput, calls=%fused_computation.130 | convolution fusion | flops 536870912 | bytes 5505024 | tf_op jit(solution)/shard_map/reshape | solution.py:153
  42.3 7.8 %collective-permute-done.1 = bf16[256,512]{0,1:T(8,128)(2,1)S(1)} collective-permute-done((bf16[256,512]{0,1:T(8,128)(2,1)S(1)}, bf16[256,512]{0,1:T(8,128)(2,1)S(1)}, u32[]{:S(2)}, u32[]{:S(2)}) %collective-permute-start.1) | collective-permute-done | bytes 262176 | tf_op jit(solution)/shard_map/ppermute | solution.py:70
  51.5 15.1 %collective-permute-done.2 = bf16[512,512]{0,1:T(8,128)(2,1)S(1)} collective-permute-done((bf16[512,512]{0,1:T(8,128)(2,1)S(1)}, bf16[512,512]{0,1:T(8,128)(2,1)S(1)}, u32[]{:S(2)}, u32[]{:S(2)}) %collective-permute-start.2) | collective-permute-done | bytes 524320 | tf_op jit(solution)/shard_map/ppermute | solution.py:70
  67.0 8.2 %convolution_bitcast_fusion = f32[16,8,16,128]{3,1,2,0:T(8,128)S(1)} fusion(bf16[128,4096]{1,0:T(8,128)(2,1)S(1)} %copy-done, bf16[4096,2048]{1,0:T(8,128)(2,1)} %param.21), kind=kOutput, calls=%fused_computation.93 | convolution fusion | flops 2147483648 | bytes 18874368 | tf_op jit(solution)/shard_map/dot_general | solution.py:140
  77.7 40.5 %collective-permute-done.3 = bf16[1024,512]{0,1:T(8,128)(2,1)S(1)} collective-permute-done((bf16[1024,512]{0,1:T(8,128)(2,1)S(1)}, bf16[1024,512]{0,1:T(8,128)(2,1)S(1)}, u32[]{:S(2)}, u32[]{:S(2)}) %collective-permute-start.3) | collective-permute-done | bytes 1048608 | tf_op jit(solution)/shard_map/ppermute | solution.py:70
  125.8 4.0 %fusion.76 = (bf16[2048,1,128]{2,1,0:T(2,128)(2,1)S(1)}, bf16[2048,1,128]{2,1,0:T(2,128)(2,1)}, bf16[2048,1,128]{2,1,0:T(2,128)(2,1)}, bf16[2048,1,128]{2,1,0:T(2,128)(2,1)S(1)}) fusion(bf16[2048,4,128]{2,1,0:T(4,128)(2,1)S(1)} %reshape.191), kind=kLoop, calls=%fused_computation.128 | loop fusion | bytes 4194304 | tf_op jit(solution)/shard_map/jit(dynamic_index_in_dim)/dynamic_slice | solution.py:83
  130.0 19.3 %while.96 = (s32[]{:T(128)}, f32[512]{0:T(512)S(1)}, f32[512]{0:T(512)S(1)}, f32[512,128]{1,0:T(8,128)S(1)}, s32[4]{0:T(128)S(1)}, /*index=5*/s32[]{:T(128)}, bf...) while((s32[]{:T(128)}, f32[512]{0:T(512)S(1)}, ...), condition=%wide.region_6.7_spmd.clone, body=%wide.region_1.6_spmd.clone.sunk | while | flops 137496064 | bytes 4121879 | solution.py:110
  131.9 2.9 %conditional.12 = ((f32[512]{0:T(512)S(1)}, f32[512]{0:T(512)S(1)}, f32[512,128]{1,0:T(8,128)S(1)})) conditional(s32[]{:T(128)} %convert_element_type.119, (f32[512]{0:T(512)S(1)}, f32[512]{0:T(512)S(1)}, f32[512,128]{1,0:T(8,128)S(1)}) %tuple.154, (s32[]{:T(128)}, s32[512]{0:T(512)S(1)}, s32[128]{0:T(128)S(1)}, bf16[4,512,128]{2,1,0:T(8,128)(2,1)}, ...), branch_computations={%region_2.2_spmd, %region_3.5_spmd} | conditional | flops 137496064 | bytes 4119592 | solution.py:100
  136.7 2.9 %conditional.12 = ((f32[512]{0:T(512)S(1)}, f32[512]{0:T(512)S(1)}, f32[512,128]{1,0:T(8,128)S(1)})) conditional(s32[]{:T(128)} %convert_element_type.119, (f32[512]{0:T(512)S(1)}, f32[512]{0:T(512)S(1)}, f32[512,128]{1,0:T(8,128)S(1)}) %tuple.154, (s32[]{:T(128)}, s32[512]{0:T(512)S(1)}, s32[128]{0:T(128)S(1)}, bf16[4,512,128]{2,1,0:T(8,128)(2,1)}, ...), branch_computations={%region_2.2_spmd, %region_3.5_spmd} | conditional | flops 137496064 | bytes 4119592 | solution.py:100
  141.5 2.9 %conditional.12 = ((f32[512]{0:T(512)S(1)}, f32[512]{0:T(512)S(1)}, f32[512,128]{1,0:T(8,128)S(1)})) conditional(s32[]{:T(128)} %convert_element_type.119, (f32[512]{0:T(512)S(1)}, f32[512]{0:T(512)S(1)}, f32[512,128]{1,0:T(8,128)S(1)}) %tuple.154, (s32[]{:T(128)}, s32[512]{0:T(512)S(1)}, s32[128]{0:T(128)S(1)}, bf16[4,512,128]{2,1,0:T(8,128)(2,1)}, ...), branch_computations={%region_2.2_spmd, %region_3.5_spmd} | conditional | flops 137496064 | bytes 4119592 | solution.py:100
  146.3 2.9 %conditional.12 = ((f32[512]{0:T(512)S(1)}, f32[512]{0:T(512)S(1)}, f32[512,128]{1,0:T(8,128)S(1)})) conditional(s32[]{:T(128)} %convert_element_type.119, (f32[512]{0:T(512)S(1)}, f32[512]{0:T(512)S(1)}, f32[512,128]{1,0:T(8,128)S(1)}) %tuple.154, (s32[]{:T(128)}, s32[512]{0:T(512)S(1)}, s32[128]{0:T(128)S(1)}, bf16[4,512,128]{2,1,0:T(8,128)(2,1)}, ...), branch_computations={%region_2.2_spmd, %region_3.5_spmd} | conditional | flops 137496064 | bytes 4119592 | solution.py:100
  149.7 19.1 %while.97 = (s32[]{:T(128)}, f32[512]{0:T(512)S(1)}, f32[512]{0:T(512)S(1)}, f32[512,128]{1,0:T(8,128)S(1)}, s32[4]{0:T(128)S(1)}, /*index=5*/s32[]{:T(128)}, bf...) while((s32[]{:T(128)}, f32[512]{0:T(512)S(1)}, ...), condition=%wide.region_12.13_spmd.clone, body=%wide.region_7.12_spmd.clone.sunk | while | flops 137496064 | bytes 4121879 | solution.py:110
  151.6 2.9 %conditional.13 = ((f32[512]{0:T(512)S(1)}, f32[512]{0:T(512)S(1)}, f32[512,128]{1,0:T(8,128)S(1)})) conditional(s32[]{:T(128)} %convert_element_type.120, (f32[512]{0:T(512)S(1)}, f32[512]{0:T(512)S(1)}, f32[512,128]{1,0:T(8,128)S(1)}) %tuple.157, (s32[]{:T(128)}, s32[512]{0:T(512)S(1)}, s32[128]{0:T(128)S(1)}, bf16[4,512,128]{2,1,0:T(8,128)(2,1)}, ...), branch_computations={%region_8.8_spmd, %region_9.11_spmd} | conditional | flops 137496064 | bytes 4119592 | solution.py:100
  156.3 2.9 %conditional.13 = ((f32[512]{0:T(512)S(1)}, f32[512]{0:T(512)S(1)}, f32[512,128]{1,0:T(8,128)S(1)})) conditional(s32[]{:T(128)} %convert_element_type.120, (f32[512]{0:T(512)S(1)}, f32[512]{0:T(512)S(1)}, f32[512,128]{1,0:T(8,128)S(1)}) %tuple.157, (s32[]{:T(128)}, s32[512]{0:T(512)S(1)}, s32[128]{0:T(128)S(1)}, bf16[4,512,128]{2,1,0:T(8,128)(2,1)}, ...), branch_computations={%region_8.8_spmd, %region_9.11_spmd} | conditional | flops 137496064 | bytes 4119592 | solution.py:100
  161.1 2.9 %conditional.13 = ((f32[512]{0:T(512)S(1)}, f32[512]{0:T(512)S(1)}, f32[512,128]{1,0:T(8,128)S(1)})) conditional(s32[]{:T(128)} %convert_element_type.120, (f32[512]{0:T(512)S(1)}, f32[512]{0:T(512)S(1)}, f32[512,128]{1,0:T(8,128)S(1)}) %tuple.157, (s32[]{:T(128)}, s32[512]{0:T(512)S(1)}, s32[128]{0:T(128)S(1)}, bf16[4,512,128]{2,1,0:T(8,128)(2,1)}, ...), branch_computations={%region_8.8_spmd, %region_9.11_spmd} | conditional | flops 137496064 | bytes 4119592 | solution.py:100
  165.9 2.9 %conditional.13 = ((f32[512]{0:T(512)S(1)}, f32[512]{0:T(512)S(1)}, f32[512,128]{1,0:T(8,128)S(1)})) conditional(s32[]{:T(128)} %convert_element_type.120, (f32[512]{0:T(512)S(1)}, f32[512]{0:T(512)S(1)}, f32[512,128]{1,0:T(8,128)S(1)}) %tuple.157, (s32[]{:T(128)}, s32[512]{0:T(512)S(1)}, s32[128]{0:T(128)S(1)}, bf16[4,512,128]{2,1,0:T(8,128)(2,1)}, ...), branch_computations={%region_8.8_spmd, %region_9.11_spmd} | conditional | flops 137496064 | bytes 4119592 | solution.py:100
  169.2 19.1 %while.98 = (s32[]{:T(128)}, f32[512]{0:T(512)S(1)}, f32[512]{0:T(512)S(1)}, f32[512,128]{1,0:T(8,128)S(1)}, s32[4]{0:T(128)S(1)}, /*index=5*/s32[]{:T(128)}, bf...) while((s32[]{:T(128)}, f32[512]{0:T(512)S(1)}, ...), condition=%wide.region_18.19_spmd.clone, body=%wide.region_13.18_spmd.clone.sunk | while | flops 137496064 | bytes 4121879 | solution.py:110
  188.6 19.1 %while.99 = (s32[]{:T(128)}, f32[512]{0:T(512)S(1)}, f32[512]{0:T(512)S(1)}, f32[512,128]{1,0:T(8,128)S(1)}, s32[4]{0:T(128)S(1)}, /*index=5*/s32[]{:T(128)}, bf...) while((s32[]{:T(128)}, f32[512]{0:T(512)S(1)}, ...), condition=%wide.region_24.25_spmd.clone, body=%wide.region_19.24_spmd.clone.sunk | while | flops 137496064 | bytes 4121879 | solution.py:110
  190.5 2.9 %conditional.15 = ((f32[512]{0:T(512)S(1)}, f32[512]{0:T(512)S(1)}, f32[512,128]{1,0:T(8,128)S(1)})) conditional(s32[]{:T(128)} %convert_element_type.122, (f32[512]{0:T(512)S(1)}, f32[512]{0:T(512)S(1)}, f32[512,128]{1,0:T(8,128)S(1)}) %tuple.163, (s32[]{:T(128)}, s32[512]{0:T(512)S(1)}, s32[128]{0:T(128)S(1)}, bf16[4,512,128]{2,1,0:T(8,128)(2,1)}, ...), branch_computations={%region_20.20_spmd, %region_21.23_spmd} | conditional | flops 137496064 | bytes 4119592 | solution.py:100
  195.2 2.9 %conditional.15 = ((f32[512]{0:T(512)S(1)}, f32[512]{0:T(512)S(1)}, f32[512,128]{1,0:T(8,128)S(1)})) conditional(s32[]{:T(128)} %convert_element_type.122, (f32[512]{0:T(512)S(1)}, f32[512]{0:T(512)S(1)}, f32[512,128]{1,0:T(8,128)S(1)}) %tuple.163, (s32[]{:T(128)}, s32[512]{0:T(512)S(1)}, s32[128]{0:T(128)S(1)}, bf16[4,512,128]{2,1,0:T(8,128)(2,1)}, ...), branch_computations={%region_20.20_spmd, %region_21.23_spmd} | conditional | flops 137496064 | bytes 4119592 | solution.py:100
  200.0 2.9 %conditional.15 = ((f32[512]{0:T(512)S(1)}, f32[512]{0:T(512)S(1)}, f32[512,128]{1,0:T(8,128)S(1)})) conditional(s32[]{:T(128)} %convert_element_type.122, (f32[512]{0:T(512)S(1)}, f32[512]{0:T(512)S(1)}, f32[512,128]{1,0:T(8,128)S(1)}) %tuple.163, (s32[]{:T(128)}, s32[512]{0:T(512)S(1)}, s32[128]{0:T(128)S(1)}, bf16[4,512,128]{2,1,0:T(8,128)(2,1)}, ...), branch_computations={%region_20.20_spmd, %region_21.23_spmd} | conditional | flops 137496064 | bytes 4119592 | solution.py:100
  204.8 2.9 %conditional.15 = ((f32[512]{0:T(512)S(1)}, f32[512]{0:T(512)S(1)}, f32[512,128]{1,0:T(8,128)S(1)})) conditional(s32[]{:T(128)} %convert_element_type.122, (f32[512]{0:T(512)S(1)}, f32[512]{0:T(512)S(1)}, f32[512,128]{1,0:T(8,128)S(1)}) %tuple.163, (s32[]{:T(128)}, s32[512]{0:T(512)S(1)}, s32[128]{0:T(128)S(1)}, bf16[4,512,128]{2,1,0:T(8,128)(2,1)}, ...), branch_computations={%region_20.20_spmd, %region_21.23_spmd} | conditional | flops 137496064 | bytes 4119592 | solution.py:100
  (247 shorter events, 84.8 us)
Async XLA Ops:
  6.5 24.7 %all-gather.3.cloned.1.call-start = ((), (), s32[]{:S(2)}) async-start(), calls=%async_computation | async-start | bytes 1572864 | tf_op jit(solution)/shard_map/all_gather | solution.py:137
  7.3 116.0 %all-gather.5.cloned.1.call-start = ((), (), s32[]{:S(2)}) async-start(), calls=%async_computation.1 | async-start | bytes 2228224 | tf_op jit(solution)/shard_map/all_gather | solution.py:75
  31.2 4.0 %copy-start = (bf16[128,4096]{1,0:T(8,128)(2,1)S(1)}, bf16[128,4096]{1,0:T(8,128)(2,1)}, u32[]{:S(2)}) copy-start(bf16[128,4096]{1,0:T(8,128)(2,1)} %all-gather.3.cloned.1.call-done) | copy-start | bytes 3145732
  39.2 1.7 collective-permute-start
  41.0 9.1 %collective-permute-start.1 = (bf16[256,512]{0,1:T(8,128)(2,1)S(1)}, bf16[256,512]{0,1:T(8,128)(2,1)S(1)}, u32[]{:S(2)}, u32[]{:S(2)}) collective-permute-start(bf16[256,512]{0,1:T(8,128)(2,1)S(1)} %maximum_select_fusion.6), channel_id=1, source_target_pairs={{0,4},{2,6},{4,0},{6,2},{8,12},{10,14},{12,8},{14,10},{16,20},{18,... | collective-permute-start | bytes 786440 | tf_op jit(solution)/shard_map/ppermute | solution.py:70
  50.3 16.3 %collective-permute-start.2 = (bf16[512,512]{0,1:T(8,128)(2,1)S(1)}, bf16[512,512]{0,1:T(8,128)(2,1)S(1)}, u32[]{:S(2)}, u32[]{:S(2)}) collective-permute-start(bf16[512,512]{0,1:T(8,128)(2,1)S(1)} %maximum_select_fusion.4), channel_id=1, source_target_pairs={{0,8},{2,10},{4,12},{6,14},{8,0},{10,2},{12,4},{14,6},{16,24},{18,... | collective-permute-start | bytes 1572872 | tf_op jit(solution)/shard_map/ppermute | solution.py:70
  66.9 51.3 %collective-permute-start.3 = (bf16[1024,512]{0,1:T(8,128)(2,1)S(1)}, bf16[1024,512]{0,1:T(8,128)(2,1)S(1)}, u32[]{:S(2)}, u32[]{:S(2)}) collective-permute-start(bf16[1024,512]{0,1:T(8,128)(2,1)S(1)} %maximum_select_fusion.2), channel_id=1, source_target_pairs={{0,16},{2,18},{4,20},{6,22},{8,24},{10,26},{12,28},{14,30},{16,0},... | collective-permute-start | bytes 3145736 | tf_op jit(solution)/shard_map/ppermute | solution.py:70
  130.0 19.6 %copy-start.2 = (bf16[2048,1,128]{2,1,0:T(2,128)(2,1)S(1)}, bf16[2048,1,128]{2,1,0:T(2,128)(2,1)}, u32[]{:S(2)}) copy-start(bf16[2048,1,128]{2,1,0:T(2,128)(2,1)} %get-tuple-element.899) | copy-start | bytes 1572868
  149.7 19.3 %copy-start.1 = (bf16[2048,1,128]{2,1,0:T(2,128)(2,1)S(1)}, bf16[2048,1,128]{2,1,0:T(2,128)(2,1)}, u32[]{:S(2)}) copy-start(bf16[2048,1,128]{2,1,0:T(2,128)(2,1)} %get-tuple-element.898) | copy-start | bytes 1572868
Sparse Core Ops, SparseCore 0:
  8.9 22.2 all-gather.2
  35.3 64.3 all-gather.4
